TPU v7x, 32 devices: a whole 2x2x4 slice. The times are simulated.
32 devices in a mesh: gx: 2 (over y), gy: 4 (over x, core), gz: 4 (over z).
Axes of the slice: x: 2, y: 2, z: 4, core: 2. Of those that a mesh axis runs over, the one named last changes fastest.
Arguments:
- fluid_state: float32 [4, 32, 64, 512], P(None, 'gx', 'gy', 'gz'), may hold values from -6 to 6
- shell_disp: float32 [3, 32768], P(None, ('gy', 'gz')), may hold values from -6 to 6
- quad_weights: float32 [32, 32, 64], P(('gx', 'gy', 'gz')), may hold values from 0.25 to 1
- quad_elements: int32 [32, 32, 64], P(('gx', 'gy', 'gz')), may hold values from 0 to 32767
- owner_cells: int32 [32, 32, 64], P(('gx', 'gy', 'gz')), may hold values from 0 to 32767
- owner_counts: int32 [32, 32], P(('gx', 'gy', 'gz')), may hold values from 0 to 64, as said below
Outputs:
- fluid_out: float32 [4, 32, 64, 512], P(None, 'gx', 'gy', 'gz')
- shell_out: float32 [3, 32768], P(None, ('gy', 'gz'))
Inputs may be any that keep to these rules, and one draw needn't show every extreme that they name: `owner_counts`: some owner has 64 live records from every sender; some owner has none from some sender.
All inputs are finite; a program needn't handle non-finite values.
Results may differ from a plain program's by a relative error of at most 0.000023.
Values sent between devices are 32-bit elements; how exact they have to be, the bound alone decides.
A program may use at most 128 MiB of HBM per device.

v0:
```python
import jax
import jax.numpy as jnp
from jax import lax
from jax.sharding import PartitionSpec as P

ITERS = 2
advection = 0.2
penalty = 0.5
relaxation = 0.05


def with_halo(cells, sides, width):
    for axis, dim in sides:
        count = lax.axis_size(axis)
        ends = count - 1
        head = lax.slice_in_dim(cells, 0, width, axis=dim)
        tail = lax.slice_in_dim(cells, cells.shape[dim] - width, cells.shape[dim], axis=dim)
        cells = jnp.concatenate(
            [
                lax.ppermute(tail, axis, [(i, (i + 1) % count) for i in range(ends)]),
                cells,
                lax.ppermute(head, axis, [((i + 1) % count, i) for i in range(ends)]),
            ],
            axis=dim,
        )
    return cells


def smooth_axis(values, axis):
    length = values.shape[axis] - 2
    lower = lax.slice_in_dim(values, 0, length, axis=axis)
    middle = lax.slice_in_dim(values, 1, length + 1, axis=axis)
    upper = lax.slice_in_dim(values, 2, length + 2, axis=axis)
    return 0.25 * lower + 0.5 * middle + 0.25 * upper


def sweep_fluid(padded):
    smoothed = smooth_axis(smooth_axis(smooth_axis(padded, 1), 2), 3)
    center = padded[:, 1:-1, 1:-1, 1:-1]
    grad_x = 0.5 * (padded[:, 2:, 1:-1, 1:-1] - padded[:, :-2, 1:-1, 1:-1])
    grad_y = 0.5 * (padded[:, 1:-1, 2:, 1:-1] - padded[:, 1:-1, :-2, 1:-1])
    grad_z = 0.5 * (padded[:, 1:-1, 1:-1, 2:] - padded[:, 1:-1, 1:-1, :-2])
    convect = center[0:1] * grad_x + center[1:2] * grad_y + center[2:3] * grad_z
    updated = smoothed - advection * convect
    pressure_grad = jnp.stack([grad_x[3], grad_y[3], grad_z[3]])
    return jnp.concatenate([updated[0:3] - advection * pressure_grad, updated[3:4]], 0)


def on_device(fluid_state, shell_disp, quad_weights, quad_elements, owner_cells, owner_counts):
    slots = quad_weights.shape[2]
    elements = quad_elements[0]
    cells_local = owner_cells[0]
    slot_index = jnp.arange(slots, dtype=jnp.int32)[None, :]
    live_mask = (slot_index < owner_counts[0][:, None]).astype(jnp.float32)
    block_shape = fluid_state.shape
    for iteration in range(ITERS):
        padded = with_halo(fluid_state, (("gx", 1), ("gy", 2), ("gz", 3)), 1)
        halfway = sweep_fluid(padded)
        all_nodes = lax.all_gather(shell_disp, ("gy", "gz"), axis=1, tiled=True)
        shell_vel = all_nodes[:, elements]
        records = jnp.concatenate([shell_vel, quad_weights[0][None]], 0)
        received = lax.all_to_all(
            records, ("gx", "gy", "gz"), split_axis=1, concat_axis=1, tiled=True
        )
        flat_vel = halfway[0:3].reshape(3, -1)
        velocity = flat_vel[:, cells_local]
        traction = penalty * received[3][None] * (velocity - received[0:3]) * live_mask[None]
        forcing = jnp.zeros_like(flat_vel).at[:, cells_local].add(traction)
        forcing = forcing.reshape(3, block_shape[1], block_shape[2], block_shape[3])
        fluid_state = jnp.concatenate([halfway[0:3] - forcing, halfway[3:4]], 0)
        returned = lax.all_to_all(
            traction, ("gx", "gy", "gz"), split_axis=1, concat_axis=1, tiled=True
        )
        node_terms = jnp.zeros((3, all_nodes.shape[1]), jnp.float32).at[:, elements].add(returned)
        partial_loads = lax.psum_scatter(node_terms, ("gy", "gz"), scatter_dimension=1, tiled=True)
        node_loads = lax.psum(partial_loads, "gx")
        shell_disp = shell_disp + relaxation * node_loads
    return (fluid_state, shell_disp)


def solution(mesh):
    return jax.shard_map(
        on_device,
        mesh=mesh,
        in_specs=(
            P(None, "gx", "gy", "gz"),
            P(None, ("gy", "gz")),
            P(("gx", "gy", "gz"), None, None),
            P(("gx", "gy", "gz"), None, None),
            P(("gx", "gy", "gz"), None, None),
            P(("gx", "gy", "gz"), None),
        ),
        out_specs=(P(None, "gx", "gy", "gz"), P(None, ("gy", "gz"))),
        check_vma=False,
    )
```

profile of v0, /device:TPU:0, one launch (start us, length us, event | category | flops | bytes accessed | tf_op | source)
XLA Modules:
  0.0 1414.3 jit_solution(13298228462873777052)
XLA Ops:
  7.2 0.8 fusion.46
  8.0 4.9 collective-permute-start
  12.8 1.3 collective-permute-start.1
  15.0 1.1 copy.153
  16.1 359.1 %all_gather.6 = f32[3,32768]{0,1:T(8,128)} all-gather(f32[3,2048]{0,1:T(8,128)S(1)} %copy.153), channel_id=1, replica_groups=mesh['gx'=2,'gy'=4,'gz'=4] {'gy','gz'}, dimensions={1}, use_global_device_ids=true | all-gather | bytes 417792 | tf_op jit(solution)/shard_map/all_gather | solution.py:59
  375.3 11.2 gather_fusion
  387.7 5.4 all-to-all-start
  394.7 2.2 collective-permute-start.2
  396.9 1.3 collective-permute-start.3
  398.2 4.2 copy.142
  403.8 4.3 copy.141
  408.1 4.3 copy.143
  412.5 8.1 pad_maximum_fusion
  420.6 2.6 copy-done.1
  423.9 4.2 collective-permute-start.4
  428.0 1.7 collective-permute-start.5
  429.8 4.6 copy.145
  435.6 1.3 copy.144
  437.0 2.3 copy.146
  439.3 1.9 pad_maximum_fusion.2
  442.6 0.9 fusion.26
  444.3 8.7 copy.157
  453.0 13.3 gather_fusion.1
  466.3 1.6 copy.158
  468.0 1.4 copy.190
  469.4 18.6 %scatter_custom_fusion = f32[3,32768]{0,1:T(8,128)} fusion(s32[2048]{0:T(1024)} %copy-done.35, f32[2048,3]{1,0:T(8,128)} %bitcast.86, f32[]{:T(128)} %constant.10.clone.1), kind=kCustom, calls=%fused_computation.14 | custom fusion | flops 6144 | bytes 393728 | tf_op jit(solution)/shard_map/scatter-add | solution.py:68
  488.0 10.0 copy.161
  498.1 3.4 collective-permute-start.6
  501.5 1.3 collective-permute-start.7
  503.5 10.1 all-to-all-start.1
  514.5 2.2 collective-permute-start.8
  516.6 1.5 collective-permute-start.9
  518.2 4.3 copy.165
  522.5 0.8 reduce.1
  523.4 4.3 copy.164
  527.6 4.2 copy.166
  531.8 8.1 pad_maximum_fusion.1
  540.0 2.6 copy-done
  542.6 3.5 collective-permute-start.10
  546.2 1.3 collective-permute-start.11
  547.5 1.4 copy.191
  548.9 18.6 %scatter_custom_fusion.1 = f32[3,32768]{0,1:T(8,128)} fusion(s32[2048]{0:T(1024)} %copy-done.34, f32[2048,3]{1,0:T(8,128)} %bitcast.87, f32[]{:T(128)} %constant.10.clone.1), kind=kCustom, calls=%fused_computation.12 | custom fusion | flops 6144 | bytes 393728 | tf_op jit(solution)/shard_map/scatter-add | solution.py:74
  567.5 4.6 copy.168
  572.8 1.5 copy.167
  574.2 1.5 copy.169
  575.7 2.2 pad_maximum_fusion.3
  579.3 1.6 fusion.20
  581.1 168.3 %reduce-scatter.3.cloned.1.call-done = f32[3,2048]{0,1:T(8,128)} async-done(((f32[3,32768]{0,1:T(8,128)}), f32[3,2048]{0,1:T(8,128)}) %reduce-scatter.3.cloned.1.call-update) | async-done | bytes 24592 | tf_op jit(solution)/shard_map/reduce_scatter | solution.py:75
  749.3 28.5 %psum.14 = f32[3,2048]{0,1:T(8,128)S(1)} all-reduce(f32[3,2048]{0,1:T(8,128)} %reduce-scatter.3.cloned.1.call-done), channel_id=1, replica_groups=mesh['gx'=2,'gy'=4,'gz'=4] {'gx'}, use_global_device_ids=true, to_apply=%region_3.0 | all-reduce | flops 6144 | bytes 49152 | tf_op jit(solution)/shard_map/psum | solution.py:76
  777.9 353.5 %all_gather.7 = f32[3,32768]{0,1:T(8,128)} all-gather(f32[3,2048]{0,1:T(8,128)S(1)} %multiply_add_fusion.1), channel_id=1, replica_groups=mesh['gx'=2,'gy'=4,'gz'=4] {'gy','gz'}, dimensions={1}, use_global_device_ids=true | all-gather | bytes 417792 | tf_op jit(solution)/shard_map/all_gather | solution.py:59
  1131.4 11.2 gather_fusion.2
  1143.8 5.2 all-to-all-start.2
  1149.1 8.7 copy.182
  1157.8 11.2 gather_fusion.3
  1169.4 0.8 reduce.2
  1171.1 5.8 all-to-all-start.3
  1177.0 7.2 all-to-all-done.3
  1185.5 18.4 %scatter_custom_fusion.3 = f32[3,32768]{0,1:T(8,128)} fusion(s32[2048]{0:T(1024)} %copy-done.34, f32[2048,3]{1,0:T(8,128)S(1)} %bitcast.85, f32[]{:T(128)} %constant.10.clone.1), kind=kCustom, calls=%fused_computation.8 | custom fusion | flops 6144 | bytes 393728 | tf_op jit(solution)/shard_map/scatter-add | solution.py:74
  1204.3 21.6 %scatter_custom_fusion.2 = f32[3,32768]{0,1:T(8,128)} fusion(s32[2048]{0:T(1024)} %copy-done.35, f32[2048,3]{1,0:T(8,128)S(1)} %bitcast.84, f32[]{:T(128)} %constant.10.clone.1), kind=kCustom, calls=%fused_computation.10 | custom fusion | flops 6144 | bytes 393728 | tf_op jit(solution)/shard_map/scatter-add | solution.py:68
  1225.9 10.3 copy.186
  1236.3 0.8 pad_maximum_fusion.25
  1237.2 140.6 %reduce-scatter.5.cloned.1.call-done = f32[3,2048]{0,1:T(8,128)} async-done(((f32[3,32768]{0,1:T(8,128)}), f32[3,2048]{0,1:T(8,128)}) %reduce-scatter.5.cloned.1.call-update) | async-done | bytes 24592 | tf_op jit(solution)/shard_map/reduce_scatter | solution.py:75
  1377.7 28.5 %psum.15 = f32[3,2048]{0,1:T(8,128)S(1)} all-reduce(f32[3,2048]{0,1:T(8,128)} %reduce-scatter.5.cloned.1.call-done), channel_id=1, replica_groups=mesh['gx'=2,'gy'=4,'gz'=4] {'gx'}, use_global_device_ids=true, to_apply=%region_7.0 | all-reduce | flops 6144 | bytes 49152 | tf_op jit(solution)/shard_map/psum | solution.py:76
  1406.3 0.9 copy.189
  (164 shorter events, 17.6 us)
Async XLA Ops:
  8.0 386.0 %collective-permute-start = (f32[4,1,16,128]{3,2,1,0:T(8,128)S(1)}, f32[4,1,16,128]{3,2,1,0:T(8,128)S(1)}, u32[]{:S(2)}, u32[]{:S(2)}) collective-permute-start(f32[4,1,16,128]{3,2,1,0:T(8,128)S(1)} %get-tuple-element.36), channel_id=1, source_target_pairs={{0,16},{1,17},{2,18},{3,19},{4,20},{5,21},{6,22},{7,23},{8,24},{9,... | collective-permute-start | bytes 98312 | tf_op jit(solution)/shard_map/ppermute | solution.py:20
  12.8 381.2 %collective-permute-start.1 = (f32[4,1,16,128]{3,2,1,0:T(8,128)S(1)}, f32[4,1,16,128]{3,2,1,0:T(8,128)S(1)}, u32[]{:S(2)}, u32[]{:S(2)}) collective-permute-start(f32[4,1,16,128]{3,2,1,0:T(8,128)S(1)} %get-tuple-element.35), channel_id=1, source_target_pairs={{16,0},{17,1},{18,2},{19,3},{20,4},{21,5},{22,6},{23,7},{24,8},{25... | collective-permute-start | bytes 98312 | tf_op jit(solution)/shard_map/ppermute | solution.py:22
  14.9 360.3 %copy-start.34 = (s32[2048]{0:T(1024)}, s32[2048]{0:T(1024)S(1)}, u32[]{:S(2)}) copy-start(s32[2048]{0:T(1024)S(1)} %reshape.111) | copy-start | bytes 24580
  15.0 360.3 %copy-start.15 = (s32[2048]{0:T(1024)}, s32[2048]{0:T(1024)S(1)}, u32[]{:S(2)}) copy-start(s32[2048]{0:T(1024)S(1)} %broadcast_clamp_fusion.1) | copy-start | bytes 24580
  16.1 370.8 %copy-start.32 = (f32[1,32,64]{2,1,0:T(8,128)S(1)}, f32[1,32,64]{2,1,0:T(8,128)}, u32[]{:S(2)}) copy-start(f32[1,32,64]{2,1,0:T(8,128)} %param.8) | copy-start | bytes 24580
  16.1 377.0 %copy-start.5 = (f32[4,16,16,128]{3,2,1,0:T(8,128)S(1)}, f32[4,16,16,128]{3,2,1,0:T(8,128)}, u32[]{:S(2)}) copy-start(f32[4,16,16,128]{3,2,1,0:T(8,128)} %param.6) | copy-start | bytes 1572868
  16.1 377.7 %copy-start.36 = (s32[1,32,64]{2,1,0:T(8,128)S(1)}, s32[1,32,64]{2,1,0:T(8,128)}, u32[]{:S(2)}) copy-start(s32[1,32,64]{2,1,0:T(8,128)} %param.10) | copy-start | bytes 24580
  16.1 377.7 %copy-start.37 = (s32[1,32]{1,0:T(1,128)S(1)}, s32[1,32]{1,0:T(1,128)}, u32[]{:S(2)}) copy-start(s32[1,32]{1,0:T(1,128)} %param.11) | copy-start | bytes 388
  387.7 14.7 %all-to-all-start = ((f32[32,1,256]{2,1,0:T(1,128)}), f32[32,1,256]{2,1,0:T(1,128)S(1)}, u32[]{:S(2)}, u32[]{:S(2)}) async-start(f32[32,1,256]{2,1,0:T(1,128)} %reshape.189), calls=%async_computation | async-start | bytes 65536 | tf_op jit(solution)/shard_map/all_to_all | solution.py:62
  393.9 8.4 copy-start.35
  393.9 2.9 copy-start.28
  394.0 0.6 copy-start.30
  394.6 13.5 copy-start.9
  394.7 9.2 collective-permute-start.2
  396.9 11.2 collective-permute-start.3
  398.2 54.8 %copy-start.17 = (s32[2048]{0:T(1024)}, s32[2048]{0:T(1024)S(1)}, u32[]{:S(2)}) copy-start(s32[2048]{0:T(1024)S(1)} %broadcast_clamp_fusion) | copy-start | bytes 24580
  403.8 8.7 copy-start.11
  420.6 2.6 copy-start.1
  423.9 11.8 collective-permute-start.4
  428.0 9.0 collective-permute-start.5
  441.2 1.2 copy-start.2
  441.2 1.3 copy-start.10
  441.2 1.3 copy-start.13
  441.2 1.4 copy-start.14
  441.2 1.3 copy-start.21
  441.2 1.3 copy-start.23
  441.2 1.3 copy-start.29
  441.3 1.3 copy-start.31
  443.4 0.8 copy-start.7
  444.3 23.6 %copy-start.12 = (f32[32,4,64]{2,1,0:T(4,128)S(1)}, f32[32,4,64]{2,1,0:T(4,128)}, u32[]{:S(2)}) copy-start(f32[32,4,64]{2,1,0:T(4,128)} %copy-done.11) | copy-start | bytes 98308
  488.0 10.0 copy-start.8
  498.1 15.6 %collective-permute-start.6 = (f32[4,1,16,128]{3,2,1,0:T(8,128)S(1)}, f32[4,1,16,128]{3,2,1,0:T(8,128)S(1)}, u32[]{:S(2)}, u32[]{:S(2)}) collective-permute-start(f32[4,1,16,128]{3,2,1,0:T(8,128)S(1)} %get-tuple-element.30), channel_id=1, source_target_pairs={{0,16},{1,17},{2,18},{3,19},{4,20},{5,21},{6,22},{7,23},{8,24},{9,... | collective-permute-start | bytes 98312 | tf_op jit(solution)/shard_map/ppermute | solution.py:20
  501.5 12.3 collective-permute-start.7
  503.5 19.0 %all-to-all-start.1 = ((f32[32,1,192]{2,1,0:T(1,128)}), f32[32,1,192]{2,1,0:T(1,128)S(1)}, u32[]{:S(2)}, u32[]{:S(2)}) async-start(f32[32,1,192]{2,1,0:T(1,128)} %reshape.191), calls=%async_computation.1 | async-start | bytes 65536 | tf_op jit(solution)/shard_map/all_to_all | solution.py:71
  513.7 235.7 %reduce-scatter.3.cloned.1.call-start = ((), (), s32[]{:S(2)}) async-start(), calls=%async_computation.6 | async-start | bytes 17825792 | tf_op jit(solution)/shard_map/reduce_scatter | solution.py:75
  513.7 13.9 copy-start.24
  513.7 0.6 copy-start.26
  514.5 8.9 collective-permute-start.8
  516.6 11.0 collective-permute-start.9
  527.6 12.3 copy-start.19
  540.0 2.6 copy-start
  542.6 30.2 %collective-permute-start.10 = (f32[4,18,18,1]{2,1,3,0:T(8,128)S(1)}, f32[4,18,18,1]{2,1,3,0:T(8,128)S(1)}, u32[]{:S(2)}, u32[]{:S(2)}) collective-permute-start(f32[4,18,18,1]{2,1,3,0:T(8,128)S(1)} %get-tuple-element.22), channel_id=1, source_target_pairs={{0,1},{1,2},{2,3},{4,5},{5,6},{6,7},{8,9},{9,10},{10,11},{12,13},{... | collective-permute-start | bytes 15560 | tf_op jit(solution)/shard_map/ppermute | solution.py:20
  546.2 28.1 %collective-permute-start.11 = (f32[4,18,18,1]{2,1,3,0:T(8,128)S(1)}, f32[4,18,18,1]{2,1,3,0:T(8,128)S(1)}, u32[]{:S(2)}, u32[]{:S(2)}) collective-permute-start(f32[4,18,18,1]{2,1,3,0:T(8,128)S(1)} %get-tuple-element.23), channel_id=1, source_target_pairs={{1,0},{2,1},{3,2},{5,4},{6,5},{7,6},{9,8},{10,9},{11,10},{13,12},{... | collective-permute-start | bytes 15560 | tf_op jit(solution)/shard_map/ppermute | solution.py:22
  567.5 4.6 copy-start.20
  577.9 1.2 copy-start.3
  577.9 1.4 copy-start.4
  577.9 1.4 copy-start.22
  577.9 1.4 copy-start.25
  577.9 1.4 copy-start.27
  777.9 353.5 %copy-start.16 = (s32[2048]{0:T(1024)S(1)}, s32[2048]{0:T(1024)}, u32[]{:S(2)}) copy-start(s32[2048]{0:T(1024)} %copy-done.15) | copy-start | bytes 24580
  777.9 365.1 %copy-start.33 = (f32[1,32,64]{2,1,0:T(8,128)S(1)}, f32[1,32,64]{2,1,0:T(8,128)}, u32[]{:S(2)}) copy-start(f32[1,32,64]{2,1,0:T(8,128)} %param.8) | copy-start | bytes 24580
  777.9 371.1 %copy-start.6 = (f32[4,16,16,128]{3,2,1,0:T(8,128)S(1)}, f32[4,16,16,128]{3,2,1,0:T(8,128)}, u32[]{:S(2)}) copy-start(f32[4,16,16,128]{3,2,1,0:T(8,128)} %get-tuple-element.14) | copy-start | bytes 1572868
  1143.8 25.6 %all-to-all-start.2 = ((f32[32,1,256]{2,1,0:T(1,128)}), f32[32,1,256]{2,1,0:T(1,128)S(1)}, u32[]{:S(2)}, u32[]{:S(2)}) async-start(f32[32,1,256]{2,1,0:T(1,128)} %reshape.193), calls=%async_computation.3 | async-start | bytes 65536 | tf_op jit(solution)/shard_map/all_to_all | solution.py:62
  1149.1 8.7 copy-start.18
  1171.1 13.1 all-to-all-start.3
  1176.9 200.8 %reduce-scatter.5.cloned.1.call-start = ((), (), s32[]{:S(2)}) async-start(), calls=%async_computation.7 | async-start | bytes 17825792 | tf_op jit(solution)/shard_map/reduce_scatter | solution.py:75
Sparse Core Ops, SparseCore 0:
  567.6 181.6 reduce-scatter.2
  1204.0 173.6 reduce-scatter.4
where the time goes:
time: 1420 us; the launch traced here: 1410 us
  blocking collectives  770 us (54%)
  waiting for transfers between devices  316 us (22%)
  local copies, waits for them, and re-layouts  151 us (11%)
  other arithmetic  107 us (8%)
  starting transfers between devices  55.2 us (4%)
  between operations  15.2 us (1%)
    all_gather x2, blocking collectives, on_device(): all_nodes = lax.all_gather(shell_disp, ('gy', 'gz'), axis=1, tiled=True)  713 us
    reduce_scatter x2, waiting for transfers between devices, on_device(): lax.psum_scatter(node_terms, ('gy', 'gz'), scatter_dimension=1, tiled=True)  309 us
    psum x2, blocking collectives, on_device(): node_loads = lax.psum(partial_loads, 'gx')  56.9 us
    scatter-add x2, other arithmetic, on_device(): forcing = jnp.zeros_like(flat_vel).at[:, cells_local].add(traction)  40.2 us
    scatter-add x2, other arithmetic, on_device(): jnp.zeros((3, all_nodes.shape[1]), jnp.float32).at[:, elements]  37 us
  transfers between devices with their start and end apart: 18, of which 3 were waited for; matrix products, arithmetic and copies ran while one was open for 9% of the time, Pallas kernels for 0%

commit v1 on v0

--- a/solution.py
+++ b/solution.py
@@ -56,7 +56,33 @@
     for iteration in range(ITERS):
         padded = with_halo(fluid_state, (("gx", 1), ("gy", 2), ("gz", 3)), 1)
         halfway = sweep_fluid(padded)
-        all_nodes = lax.all_gather(shell_disp, ("gy", "gz"), axis=1, tiled=True)
+        answer = lax.axis_size(("gy", "gz"))
+        current_block = lax.axis_index(("gy", "gz"))
+        outer, y1, state_next = (answer, current_block, shell_disp.shape[1])
+        history = [h * outer if dev_j == 1 else h for dev_j, h in enumerate(shell_disp.shape)]
+        h_now = jnp.zeros(history, shell_disp.dtype)
+        all_nodes = lax.dynamic_update_slice_in_dim(h_now, shell_disp, y1 * state_next, axis=1)
+        res = back = shell_disp
+        p = 1
+        while p < outer // 2 + 1:
+            res = lax.ppermute(
+                res,
+                axis_name=("gy", "gz"),
+                perm=[(dev_j, (dev_j + 1) % outer) for dev_j in range(outer)],
+            )
+            all_nodes = lax.dynamic_update_slice_in_dim(
+                all_nodes, res, (y1 - p) % outer * state_next, axis=1
+            )
+            if 2 * p < outer:
+                back = lax.ppermute(
+                    back,
+                    axis_name=("gy", "gz"),
+                    perm=[(dev_j, (dev_j - 1) % outer) for dev_j in range(outer)],
+                )
+                all_nodes = lax.dynamic_update_slice_in_dim(
+                    all_nodes, back, (y1 + p) % outer * state_next, axis=1
+                )
+            p = p + 1
         shell_vel = all_nodes[:, elements]
         records = jnp.concatenate([shell_vel, quad_weights[0][None]], 0)
         received = lax.all_to_all(

time: 1420 us -> 845 us (0.60)
  blocking collectives: 770 us -> 57.3 us
  local copies, waits for them, and re-layouts: 151 us -> 210 us
  starting transfers between devices: 55.2 us -> 110 us
    all_gather x2 -> x0, blocking collectives: 713 us -> none  [on_device(): all_nodes = lax.all_gather(shell_disp, ('gy', 'gz'), axis=1, tiled=True)]
    ppermute x0 -> x30, starting transfers between devices: none -> 63.8 us  [the longest x14 57.2 us: on_device(): lax.ppermute(back, axis_name=('gy', 'gz'), perm=[(dev_j, (dev_j - 1) % ou...]
    dynamic_update_slice x0 -> x31, local copies, waits for them, and re-layouts: none -> 35.4 us  [the longest x16 18.2 us: on_device(): lax.dynamic_update_slice_in_dim(all_nodes, res, (y1 - p) % outer * state_...]
    ppermute x0 -> x30, local copies, waits for them, and re-layouts: none -> 16.6 us  [the longest x16 9.06 us: on_device(): lax.ppermute(res, axis_name=('gy', 'gz'), perm=[(dev_j, (dev_j + 1) % out...]
  transfers between devices with their start and end apart: 18 -> 48, of which waited for: 3 -> 17; matrix products, arithmetic and copies ran while one was open for 9% -> 26% of each run, Pallas kernels for 0% -> 0%
where the time goes in v1:
time: 845 us; the launch traced here: 835 us
  waiting for transfers between devices  327 us (39%)
  local copies, waits for them, and re-layouts  210 us (25%)
  other arithmetic  115 us (14%)
  starting transfers between devices  110 us (13%)
  blocking collectives  57.3 us (7%)
  between operations  15.3 us (2%)
    reduce_scatter x2, waiting for transfers between devices, on_device(): lax.psum_scatter(node_terms, ('gy', 'gz'), scatter_dimension=1, tiled=True)  308 us
    psum x2, blocking collectives, on_device(): node_loads = lax.psum(partial_loads, 'gx')  57.3 us
    ppermute x14, starting transfers between devices, on_device(): lax.ppermute(back, axis_name=('gy', 'gz'), perm=[(dev_j, (dev_j - 1) % ou...  57.2 us
    scatter-add x2, other arithmetic, on_device(): forcing = jnp.zeros_like(flat_vel).at[:, cells_local].add(traction)  40 us
    scatter-add x2, other arithmetic, on_device(): jnp.zeros((3, all_nodes.shape[1]), jnp.float32).at[:, elements]  37.1 us
    gather x4, local copies, waits for them, and re-layouts, on_device(): velocity = flat_vel[:, cells_local]  23.2 us
    gather x4, local copies, waits for them, and re-layouts, on_device(): shell_vel = all_nodes[:, elements]  23.2 us
    concatenate x5, other arithmetic, with_halo(): jnp.concatenate([lax.ppermute(tail, axis, [(i, (i + 1) % count) for i in...  20.4 us
  transfers between devices with their start and end apart: 48, of which 17 were waited for; matrix products, arithmetic and copies ran while one was open for 26% of the time, Pallas kernels for 0%

profile of v1, /device:TPU:0, one launch (start us, length us, event | category | flops | bytes accessed | tf_op | source)
XLA Modules:
  0.0 834.6 jit_solution(13883432602989787862)
XLA Ops:
  7.2 3.1 collective-permute-start.6
  10.3 2.5 collective-permute-start.7
  13.5 3.8 collective-permute-start
  24.5 6.0 broadcast.119.clone
  34.4 4.4 collective-permute-start.9
  40.2 4.1 copy.242
  50.5 4.4 collective-permute-start.11
  55.0 4.1 copy.241
  59.1 4.2 copy.243
  63.3 8.1 pad_maximum_fusion
  71.4 2.7 copy-done.1
  74.7 4.6 copy.245
  83.8 2.1 copy.258
  85.9 2.3 constant_dynamic-update-slice_fusion.26
  88.2 2.1 copy.259
  90.3 2.3 constant_dynamic-update-slice_fusion.25
  92.6 2.7 collective-permute-start.12
  98.4 2.3 copy.246
  103.1 3.3 fusion.26
  111.1 4.2 collective-permute-start.15
  118.7 4.4 collective-permute-start.17
  126.1 4.6 collective-permute-start.19
  133.8 4.5 collective-permute-done.20
  139.7 11.2 %gather_fusion = f32[2048,3]{1,0:T(8,128)S(1)} fusion(f32[3,32768]{0,1:T(8,128)} %constant_dynamic-update-slice_fusion.16, s32[2048]{0:T(1024)S(1)} %broadcast_clamp_fusion.1), kind=kCustom, calls=%fused_computation | custom fusion | bytes 57344 | tf_op jit(solution)/shard_map/gather | solution.py:86
  152.1 6.8 all-to-all-start
  159.0 8.7 %copy.272 = f32[3,16,16,128]{0,3,2,1:T(8,128)} copy(f32[3,16,16,128]{3,2,1,0:T(8,128)S(1)} %slice_subtract_fusion.1) | data formatting | bytes 786432 | tf_op jit(solution)/shard_map/sub | solution.py:46
  167.7 11.2 %gather_fusion.1 = f32[2048,3]{1,0:T(8,128)S(1)} fusion(f32[3,32768]{0,1:T(8,128)} %bitcast.79, s32[2048]{0:T(1024)S(1)} %broadcast_clamp_fusion), kind=kCustom, calls=%fused_computation.1 | custom fusion | bytes 57344 | tf_op jit(solution)/shard_map/gather | solution.py:92
  181.1 18.4 %scatter_custom_fusion = f32[3,32768]{0,1:T(8,128)} fusion(s32[2048]{0:T(1024)} %copy-done.16, f32[2048,3]{1,0:T(8,128)S(1)} %bitcast.86, f32[]{:T(128)} %constant.136.clone.1), kind=kCustom, calls=%fused_computation.14 | custom fusion | flops 6144 | bytes 393728 | tf_op jit(solution)/shard_map/scatter-add | solution.py:94
  199.5 10.0 %copy.276 = f32[3,16,16,128]{3,2,1,0:T(8,128)S(1)} copy(f32[3,16,16,128]{0,3,2,1:T(8,128)} %bitcast.77) | data formatting | bytes 786432 | tf_op jit(solution)/shard_map/reshape | solution.py:95
  209.6 3.7 collective-permute-start.21
  215.3 6.7 all-to-all-start.1
  223.4 2.2 collective-permute-start.23
  227.1 4.2 copy.280
  232.2 4.2 copy.279
  236.4 4.2 copy.281
  240.6 8.1 pad_maximum_fusion.1
  248.7 2.7 copy-done
  251.4 3.5 collective-permute-start.25
  257.7 18.6 %scatter_custom_fusion.1 = f32[3,32768]{0,1:T(8,128)} fusion(s32[2048]{0:T(1024)} %copy-done.17, f32[2048,3]{1,0:T(8,128)} %bitcast.87, f32[]{:T(128)} %constant.136.clone.1), kind=kCustom, calls=%fused_computation.12 | custom fusion | flops 6144 | bytes 393728 | tf_op jit(solution)/shard_map/scatter-add | solution.py:100
  276.3 4.6 copy.283
  284.5 2.2 pad_maximum_fusion.3
  287.2 3.2 fusion.20
  290.4 167.7 %reduce-scatter.3.cloned.1.call-done = f32[3,2048]{0,1:T(8,128)} async-done(((f32[3,32768]{0,1:T(8,128)}), f32[3,2048]{0,1:T(8,128)}) %reduce-scatter.3.cloned.1.call-update) | async-done | bytes 24592 | tf_op jit(solution)/shard_map/reduce_scatter | solution.py:101
  458.1 28.9 %psum.14 = f32[3,2048]{0,1:T(8,128)S(1)} all-reduce(f32[3,2048]{0,1:T(8,128)} %reduce-scatter.3.cloned.1.call-done), channel_id=1, replica_groups=mesh['gx'=2,'gy'=4,'gz'=4] {'gx'}, use_global_device_ids=true, to_apply=%region_3.4 | all-reduce | flops 6144 | bytes 49152 | tf_op jit(solution)/shard_map/psum | solution.py:102
  487.0 6.0 broadcast.119
  495.7 4.2 collective-permute-start.28
  503.4 4.4 collective-permute-start.30
  510.9 4.5 collective-permute-start.32
  518.4 4.4 collective-permute-start.34
  525.9 4.4 collective-permute-start.36
  533.4 4.4 collective-permute-start.38
  540.9 4.5 collective-permute-start.40
  548.5 4.4 collective-permute-done.41
  554.3 11.2 %gather_fusion.2 = f32[2048,3]{1,0:T(8,128)S(1)} fusion(f32[3,32768]{0,1:T(8,128)} %constant_dynamic-update-slice_fusion, s32[2048]{0:T(1024)S(1)} %broadcast_clamp_fusion.1), kind=kCustom, calls=%fused_computation.2 | custom fusion | bytes 57344 | tf_op jit(solution)/shard_map/gather | solution.py:86
  566.7 2.6 all-to-all-start.2
  569.4 8.7 %copy.314 = f32[3,16,16,128]{0,3,2,1:T(8,128)} copy(f32[3,16,16,128]{3,2,1,0:T(8,128)S(1)} %slice_subtract_fusion) | data formatting | bytes 786432 | tf_op jit(solution)/shard_map/sub | solution.py:46
  578.0 11.2 %gather_fusion.3 = f32[2048,3]{1,0:T(8,128)S(1)} fusion(f32[3,32768]{0,1:T(8,128)} %bitcast.78, s32[2048]{0:T(1024)S(1)} %broadcast_clamp_fusion), kind=kCustom, calls=%fused_computation.3 | custom fusion | bytes 57344 | tf_op jit(solution)/shard_map/gather | solution.py:92
  591.3 5.8 all-to-all-start.3
  597.2 7.2 all-to-all-done.3
  605.6 18.5 %scatter_custom_fusion.3 = f32[3,32768]{0,1:T(8,128)} fusion(s32[2048]{0:T(1024)} %copy-done.17, f32[2048,3]{1,0:T(8,128)S(1)} %bitcast.85, f32[]{:T(128)} %constant.136.clone.1), kind=kCustom, calls=%fused_computation.8 | custom fusion | flops 6144 | bytes 393728 | tf_op jit(solution)/shard_map/scatter-add | solution.py:100
  624.6 21.6 %scatter_custom_fusion.2 = f32[3,32768]{0,1:T(8,128)} fusion(s32[2048]{0:T(1024)} %copy-done.16, f32[2048,3]{1,0:T(8,128)S(1)} %bitcast.84, f32[]{:T(128)} %constant.136.clone.1), kind=kCustom, calls=%fused_computation.10 | custom fusion | flops 6144 | bytes 393728 | tf_op jit(solution)/shard_map/scatter-add | solution.py:94
  646.3 10.3 %copy.318 = f32[3,16,16,128]{3,2,1,0:T(8,128)S(1)} copy(f32[3,16,16,128]{0,3,2,1:T(8,128)} %bitcast.76) | data formatting | bytes 786432 | tf_op jit(solution)/shard_map/reshape | solution.py:95
  657.5 140.6 %reduce-scatter.5.cloned.1.call-done = f32[3,2048]{0,1:T(8,128)} async-done(((f32[3,32768]{0,1:T(8,128)}), f32[3,2048]{0,1:T(8,128)}) %reduce-scatter.5.cloned.1.call-update) | async-done | bytes 24592 | tf_op jit(solution)/shard_map/reduce_scatter | solution.py:101
  798.1 28.5 %psum.15 = f32[3,2048]{0,1:T(8,128)S(1)} all-reduce(f32[3,2048]{0,1:T(8,128)} %reduce-scatter.5.cloned.1.call-done), channel_id=1, replica_groups=mesh['gx'=2,'gy'=4,'gz'=4] {'gx'}, use_global_device_ids=true, to_apply=%region_7.8 | all-reduce | flops 6144 | bytes 49152 | tf_op jit(solution)/shard_map/psum | solution.py:102
  (246 shorter events, 94.2 us)
Async XLA Ops:
  7.2 31.7 %copy-start.2 = (f32[4,16,16,128]{3,2,1,0:T(8,128)S(1)}, f32[4,16,16,128]{3,2,1,0:T(8,128)}, u32[]{:S(2)}) copy-start(f32[4,16,16,128]{3,2,1,0:T(8,128)} %param.6) | copy-start | bytes 1572868
  7.2 24.4 %collective-permute-start.6 = (f32[3,2048]{1,0:T(4,128)}, f32[3,2048]{1,0:T(4,128)S(1)}, u32[]{:S(2)}, u32[]{:S(2)}) collective-permute-start(f32[3,2048]{1,0:T(4,128)} %param.7), channel_id=1, source_target_pairs={{0,1},{1,2},{2,3},{3,4},{4,5},{5,6},{6,7},{7,8},{8,9},{9,10},{10,1... | collective-permute-start | bytes 73736 | tf_op jit(solution)/shard_map/ppermute | solution.py:68
  10.3 22.7 %collective-permute-start.7 = (f32[3,2048]{1,0:T(4,128)}, f32[3,2048]{1,0:T(4,128)S(1)}, u32[]{:S(2)}, u32[]{:S(2)}) collective-permute-start(f32[3,2048]{1,0:T(4,128)} %param.7), channel_id=1, source_target_pairs={{0,15},{1,0},{2,1},{3,2},{4,3},{5,4},{6,5},{7,6},{8,7},{9,8},{10,9... | collective-permute-start | bytes 73736 | tf_op jit(solution)/shard_map/ppermute | solution.py:77
  13.5 25.4 %collective-permute-start = (f32[4,1,16,128]{3,2,1,0:T(8,128)S(1)}, f32[4,1,16,128]{3,2,1,0:T(8,128)S(1)}, u32[]{:S(2)}, u32[]{:S(2)}) collective-permute-start(f32[4,1,16,128]{3,2,1,0:T(8,128)S(1)} %get-tuple-element.38), channel_id=1, source_target_pairs={{0,16},{1,17},{2,18},{3,19},{4,20},{5,21},{6,22},{7,23},{8,24},{9,... | collective-permute-start | bytes 98312 | tf_op jit(solution)/shard_map/ppermute | solution.py:20
  17.4 21.6 %collective-permute-start.1 = (f32[4,1,16,128]{3,2,1,0:T(8,128)S(1)}, f32[4,1,16,128]{3,2,1,0:T(8,128)S(1)}, u32[]{:S(2)}, u32[]{:S(2)}) collective-permute-start(f32[4,1,16,128]{3,2,1,0:T(8,128)S(1)} %get-tuple-element.37), channel_id=1, source_target_pairs={{16,0},{17,1},{18,2},{19,3},{20,4},{21,5},{22,6},{23,7},{24,8},{25... | collective-permute-start | bytes 98312 | tf_op jit(solution)/shard_map/ppermute | solution.py:22
  23.7 10.7 %copy-start.16 = (s32[2048]{0:T(1024)}, s32[2048]{0:T(1024)S(1)}, u32[]{:S(2)}) copy-start(s32[2048]{0:T(1024)S(1)} %reshape.143) | copy-start | bytes 24580
  34.4 12.5 %collective-permute-start.8 = (f32[3,2048]{1,0:T(4,128)S(1)}, f32[3,2048]{1,0:T(4,128)}, u32[]{:S(2)}, u32[]{:S(2)}) collective-permute-start(f32[3,2048]{1,0:T(4,128)S(1)} %collective-permute-done.6), channel_id=1, source_target_pairs={{0,1},{1,2},{2,3},{3,4},{4,5},{5,6},{6,7},{7,8},{8,9},{9,10},{10,1... | collective-permute-start | bytes 73736 | tf_op jit(solution)/shard_map/ppermute | solution.py:68
  34.4 14.7 %collective-permute-start.9 = (f32[3,2048]{1,0:T(4,128)S(1)}, f32[3,2048]{1,0:T(4,128)S(1)}, u32[]{:S(2)}, u32[]{:S(2)}) collective-permute-start(f32[3,2048]{1,0:T(4,128)S(1)} %collective-permute-done.7), channel_id=1, source_target_pairs={{0,15},{1,0},{2,1},{3,2},{4,3},{5,4},{6,5},{7,6},{8,7},{9,8},{10,9... | collective-permute-start | bytes 73736 | tf_op jit(solution)/shard_map/ppermute | solution.py:77
  38.9 0.6 copy-start.12
  39.5 0.6 copy-start.14
  40.1 31.3 %copy-start.5 = (f32[4,18,16,128]{3,2,1,0:T(8,128)}, f32[4,18,16,128]{3,2,1,0:T(8,128)S(1)}, u32[]{:S(2)}) copy-start(f32[4,18,16,128]{3,2,1,0:T(8,128)S(1)} %constant_dynamic-update-slice_fusion.32) | copy-start | bytes 1769476
  44.3 10.7 %collective-permute-start.2 = (f32[4,18,1,128]{3,1,2,0:T(8,128)S(1)}, f32[4,18,1,128]{3,1,2,0:T(8,128)S(1)}, u32[]{:S(2)}, u32[]{:S(2)}) collective-permute-start(f32[4,18,1,128]{3,1,2,0:T(8,128)S(1)} %copy.330), channel_id=1, source_target_pairs={{0,4},{4,8},{8,12},{1,5},{5,9},{9,13},{2,6},{6,10},{10,14},{3,7},{... | collective-permute-start | bytes 110600 | tf_op jit(solution)/shard_map/ppermute | solution.py:20
  45.6 13.5 %collective-permute-start.3 = (f32[4,18,1,128]{3,1,2,0:T(8,128)S(1)}, f32[4,18,1,128]{3,1,2,0:T(8,128)S(1)}, u32[]{:S(2)}, u32[]{:S(2)}) collective-permute-start(f32[4,18,1,128]{3,1,2,0:T(8,128)S(1)} %copy.331), channel_id=1, source_target_pairs={{4,0},{8,4},{12,8},{5,1},{9,5},{13,9},{6,2},{10,6},{14,10},{7,3},{... | collective-permute-start | bytes 110600 | tf_op jit(solution)/shard_map/ppermute | solution.py:22
  50.5 33.3 %collective-permute-start.10 = (f32[3,2048]{1,0:T(4,128)}, f32[3,2048]{1,0:T(4,128)}, u32[]{:S(2)}, u32[]{:S(2)}) collective-permute-start(f32[3,2048]{1,0:T(4,128)} %collective-permute-done.8), channel_id=1, source_target_pairs={{0,1},{1,2},{2,3},{3,4},{4,5},{5,6},{6,7},{7,8},{8,9},{9,10},{10,1... | collective-permute-start | bytes 73736 | tf_op jit(solution)/shard_map/ppermute | solution.py:68
  50.5 37.7 %collective-permute-start.11 = (f32[3,2048]{1,0:T(4,128)S(1)}, f32[3,2048]{1,0:T(4,128)}, u32[]{:S(2)}, u32[]{:S(2)}) collective-permute-start(f32[3,2048]{1,0:T(4,128)S(1)} %collective-permute-done.9), channel_id=1, source_target_pairs={{0,15},{1,0},{2,1},{3,2},{4,3},{5,4},{6,5},{7,6},{8,7},{9,8},{10,9... | collective-permute-start | bytes 73736 | tf_op jit(solution)/shard_map/ppermute | solution.py:77
  71.4 2.7 copy-start.1
  74.1 29.0 %copy-start.6 = (f32[16,16,128]{2,1,0:T(8,128)S(1)}, f32[16,16,128]{2,1,0:T(8,128)}, u32[]{:S(2)}) copy-start(f32[16,16,128]{2,1,0:T(8,128)} %get-tuple-element.34) | copy-start | bytes 393220
  74.1 29.0 %copy-start.13 = (f32[4,1,16,128]{3,2,1,0:T(8,128)S(1)}, f32[4,1,16,128]{3,2,1,0:T(8,128)}, u32[]{:S(2)}) copy-start(f32[4,1,16,128]{3,2,1,0:T(8,128)} %copy-done.12) | copy-start | bytes 98308
  79.3 17.7 %collective-permute-start.4 = (f32[4,18,18,1]{2,1,3,0:T(8,128)S(1)}, f32[4,18,18,1]{2,1,3,0:T(8,128)}, u32[]{:S(2)}, u32[]{:S(2)}) collective-permute-start(f32[4,18,18,1]{2,1,3,0:T(8,128)S(1)} %get-tuple-element.26), channel_id=1, source_target_pairs={{0,1},{1,2},{2,3},{4,5},{5,6},{6,7},{8,9},{9,10},{10,11},{12,13},{... | collective-permute-start | bytes 15560 | tf_op jit(solution)/shard_map/ppermute | solution.py:20
  81.2 17.2 %collective-permute-start.5 = (f32[4,18,18,1]{2,1,3,0:T(8,128)}, f32[4,18,18,1]{2,1,3,0:T(8,128)}, u32[]{:S(2)}, u32[]{:S(2)}) collective-permute-start(f32[4,18,18,1]{2,1,3,0:T(8,128)} %get-tuple-element.27), channel_id=1, source_target_pairs={{1,0},{2,1},{3,2},{5,4},{6,5},{7,6},{9,8},{10,9},{11,10},{13,12},{... | collective-permute-start | bytes 15560 | tf_op jit(solution)/shard_map/ppermute | solution.py:22
  92.6 13.8 %collective-permute-start.12 = (f32[3,2048]{1,0:T(4,128)}, f32[3,2048]{1,0:T(4,128)}, u32[]{:S(2)}, u32[]{:S(2)}) collective-permute-start(f32[3,2048]{1,0:T(4,128)} %collective-permute-done.10), channel_id=1, source_target_pairs={{0,1},{1,2},{2,3},{3,4},{4,5},{5,6},{6,7},{7,8},{8,9},{9,10},{10,1... | collective-permute-start | bytes 73736 | tf_op jit(solution)/shard_map/ppermute | solution.py:68
  95.3 13.7 %collective-permute-start.13 = (f32[3,2048]{1,0:T(4,128)}, f32[3,2048]{1,0:T(4,128)}, u32[]{:S(2)}, u32[]{:S(2)}) collective-permute-start(f32[3,2048]{1,0:T(4,128)} %collective-permute-done.11), channel_id=1, source_target_pairs={{0,15},{1,0},{2,1},{3,2},{4,3},{5,4},{6,5},{7,6},{8,7},{9,8},{10,9... | collective-permute-start | bytes 73736 | tf_op jit(solution)/shard_map/ppermute | solution.py:77
  106.4 44.9 %copy-start.15 = (f32[1,32,64]{2,1,0:T(8,128)S(1)}, f32[1,32,64]{2,1,0:T(8,128)}, u32[]{:S(2)}) copy-start(f32[1,32,64]{2,1,0:T(8,128)} %param.8) | copy-start | bytes 24580
  106.4 52.5 %copy-start.4 = (f32[4,16,16,128]{3,2,1,0:T(8,128)S(1)}, f32[4,16,16,128]{3,2,1,0:T(8,128)}, u32[]{:S(2)}) copy-start(f32[4,16,16,128]{3,2,1,0:T(8,128)} %get-tuple-element.20) | copy-start | bytes 1572868
  108.7 6.6 collective-permute-start.14
  111.1 6.1 collective-permute-start.15
  116.8 6.3 collective-permute-start.16
  118.7 6.0 collective-permute-start.17
  124.5 6.4 collective-permute-start.18
  126.1 6.2 collective-permute-start.19
  132.3 6.0 collective-permute-start.20
  152.1 27.2 %all-to-all-start = ((f32[32,1,256]{2,1,0:T(1,128)}), f32[32,1,256]{2,1,0:T(1,128)S(1)}, u32[]{:S(2)}, u32[]{:S(2)}) async-start(f32[32,1,256]{2,1,0:T(1,128)} %reshape.189), calls=%async_computation | async-start | bytes 65536 | tf_op jit(solution)/shard_map/all_to_all | solution.py:88
  209.6 12.5 %collective-permute-start.21 = (f32[4,1,16,128]{3,2,1,0:T(8,128)S(1)}, f32[4,1,16,128]{3,2,1,0:T(8,128)S(1)}, u32[]{:S(2)}, u32[]{:S(2)}) collective-permute-start(f32[4,1,16,128]{3,2,1,0:T(8,128)S(1)} %get-tuple-element.32), channel_id=1, source_target_pairs={{0,16},{1,17},{2,18},{3,19},{4,20},{5,21},{6,22},{7,23},{8,24},{9,... | collective-permute-start | bytes 98312 | tf_op jit(solution)/shard_map/ppermute | solution.py:20
  213.2 8.8 %collective-permute-start.22 = (f32[4,1,16,128]{3,2,1,0:T(8,128)S(1)}, f32[4,1,16,128]{3,2,1,0:T(8,128)S(1)}, u32[]{:S(2)}, u32[]{:S(2)}) collective-permute-start(f32[4,1,16,128]{3,2,1,0:T(8,128)S(1)} %get-tuple-element.33), channel_id=1, source_target_pairs={{16,0},{17,1},{18,2},{19,3},{20,4},{21,5},{22,6},{23,7},{24,8},{25... | collective-permute-start | bytes 98312 | tf_op jit(solution)/shard_map/ppermute | solution.py:22
  215.3 16.1 %all-to-all-start.1 = ((f32[32,1,192]{2,1,0:T(1,128)}), f32[32,1,192]{2,1,0:T(1,128)S(1)}, u32[]{:S(2)}, u32[]{:S(2)}) async-start(f32[32,1,192]{2,1,0:T(1,128)} %reshape.191), calls=%async_computation.1 | async-start | bytes 65536 | tf_op jit(solution)/shard_map/all_to_all | solution.py:97
  222.0 236.1 %reduce-scatter.3.cloned.1.call-start = ((), (), s32[]{:S(2)}) async-start(), calls=%async_computation.6 | async-start | bytes 17825792 | tf_op jit(solution)/shard_map/reduce_scatter | solution.py:101
  222.1 0.6 copy-start.10
  223.4 8.8 %collective-permute-start.23 = (f32[4,18,1,128]{3,1,2,0:T(8,128)S(1)}, f32[4,18,1,128]{3,1,2,0:T(8,128)S(1)}, u32[]{:S(2)}, u32[]{:S(2)}) collective-permute-start(f32[4,18,1,128]{3,1,2,0:T(8,128)S(1)} %copy.333), channel_id=1, source_target_pairs={{0,4},{4,8},{8,12},{1,5},{5,9},{9,13},{2,6},{6,10},{10,14},{3,7},{... | collective-permute-start | bytes 110600 | tf_op jit(solution)/shard_map/ppermute | solution.py:20
  225.6 10.8 %collective-permute-start.24 = (f32[4,18,1,128]{3,1,2,0:T(8,128)S(1)}, f32[4,18,1,128]{3,1,2,0:T(8,128)S(1)}, u32[]{:S(2)}, u32[]{:S(2)}) collective-permute-start(f32[4,18,1,128]{3,1,2,0:T(8,128)S(1)} %copy.334), channel_id=1, source_target_pairs={{4,0},{8,4},{12,8},{5,1},{9,5},{13,9},{6,2},{10,6},{14,10},{7,3},{... | collective-permute-start | bytes 110600 | tf_op jit(solution)/shard_map/ppermute | solution.py:22
  236.4 39.8 %copy-start.7 = (f32[4,18,1,128]{3,1,2,0:T(8,128)}, f32[4,18,1,128]{3,1,2,0:T(8,128)S(1)}, u32[]{:S(2)}) copy-start(f32[4,18,1,128]{3,1,2,0:T(8,128)S(1)} %collective-permute-done.24) | copy-start | bytes 110596
  248.7 2.7 copy-start
  251.4 30.2 %collective-permute-start.25 = (f32[4,18,18,1]{2,1,3,0:T(8,128)S(1)}, f32[4,18,18,1]{2,1,3,0:T(8,128)S(1)}, u32[]{:S(2)}, u32[]{:S(2)}) collective-permute-start(f32[4,18,18,1]{2,1,3,0:T(8,128)S(1)} %get-tuple-element.24), channel_id=1, source_target_pairs={{0,1},{1,2},{2,3},{4,5},{5,6},{6,7},{8,9},{9,10},{10,11},{12,13},{... | collective-permute-start | bytes 15560 | tf_op jit(solution)/shard_map/ppermute | solution.py:20
  255.0 28.1 %collective-permute-start.26 = (f32[4,18,18,1]{2,1,3,0:T(8,128)S(1)}, f32[4,18,18,1]{2,1,3,0:T(8,128)S(1)}, u32[]{:S(2)}, u32[]{:S(2)}) collective-permute-start(f32[4,18,18,1]{2,1,3,0:T(8,128)S(1)} %get-tuple-element.25), channel_id=1, source_target_pairs={{1,0},{2,1},{3,2},{5,4},{6,5},{7,6},{9,8},{10,9},{11,10},{13,12},{... | collective-permute-start | bytes 15560 | tf_op jit(solution)/shard_map/ppermute | solution.py:22
  276.3 4.6 copy-start.8
  281.6 5.7 copy-start.9
  494.5 6.1 collective-permute-start.27
  495.7 6.3 collective-permute-start.28
  502.0 6.1 collective-permute-start.29
  503.4 6.1 collective-permute-start.30
  509.5 6.1 collective-permute-start.31
  510.9 6.1 collective-permute-start.32
  517.0 52.3 %copy-start.3 = (f32[4,16,16,128]{3,2,1,0:T(8,128)S(1)}, f32[4,16,16,128]{3,2,1,0:T(8,128)}, u32[]{:S(2)}) copy-start(f32[4,16,16,128]{3,2,1,0:T(8,128)} %get-tuple-element.16) | copy-start | bytes 1572868
  517.0 6.0 collective-permute-start.33
  518.4 6.0 collective-permute-start.34
  524.4 6.0 collective-permute-start.35
  525.9 6.1 collective-permute-start.36
  532.0 6.1 collective-permute-start.37
  533.4 6.0 collective-permute-start.38
  539.4 6.0 collective-permute-start.39
  540.9 6.1 collective-permute-start.40
  546.9 6.0 collective-permute-start.41
  566.7 22.9 %all-to-all-start.2 = ((f32[32,1,256]{2,1,0:T(1,128)}), f32[32,1,256]{2,1,0:T(1,128)S(1)}, u32[]{:S(2)}, u32[]{:S(2)}) async-start(f32[32,1,256]{2,1,0:T(1,128)} %reshape.193), calls=%async_computation.3 | async-start | bytes 65536 | tf_op jit(solution)/shard_map/all_to_all | solution.py:88
  591.3 13.1 %all-to-all-start.3 = ((f32[32,1,192]{2,1,0:T(1,128)}), f32[32,1,192]{2,1,0:T(1,128)S(1)}, u32[]{:S(2)}, u32[]{:S(2)}) async-start(f32[32,1,192]{2,1,0:T(1,128)} %reshape.195), calls=%async_computation.4 | async-start | bytes 65536 | tf_op jit(solution)/shard_map/all_to_all | solution.py:97
  597.1 200.9 %reduce-scatter.5.cloned.1.call-start = ((), (), s32[]{:S(2)}) async-start(), calls=%async_computation.7 | async-start | bytes 17825792 | tf_op jit(solution)/shard_map/reduce_scatter | solution.py:101
  (2 other events, 1.2 us)
Sparse Core Ops, SparseCore 0:
  276.4 181.6 reduce-scatter.2
  624.3 173.6 reduce-scatter.4
